TPU v7x, 256 devices: a whole 4x4x8 slice. The times are simulated.
256 devices in a mesh: sect: 4 (over y), pass: 16 (over z, core), qry: 4 (over x).
Axes of the slice: x: 4, y: 4, z: 8, core: 2. Of those that a mesh axis runs over, the one named last changes fastest.
Arguments:
- query_emb: bfloat16 [8192, 4096], P(('sect', 'qry')), may hold values from -0.2 to 0.2
- passage_emb: bfloat16 [16384, 4096], P(('sect', 'pass')), may hold values from -0.2 to 0.2
- block_ids: int32 [32, 64], P(('sect', 'qry')), may hold values from 0 to 255, as said below
- positives: int32 [8192], P(('sect', 'qry')), may hold values from 0 to 16383, as said below
Outputs:
- query_grad: bfloat16 [8192, 4096], P(('sect', 'qry'), 'pass')
- pool_grad: bfloat16 [16384, 4096], P(('sect', 'pass', 'qry'))
Inputs may be any that keep to these rules, and one draw needn't show every extreme that they name: `block_ids`: each row names 64 different passage blocks. `positives`: the positive passage of a query lies in a block that its query block's row of block_ids names.
All inputs are finite; a program needn't handle non-finite values.
Results may differ from a plain program's by a relative error of at most 0.015.
Values may be sent and summed in bfloat16 or wider, within the bound.
A program may use at most 128 MiB of HBM per device.

v0:
```python
import jax
import jax.numpy as jnp
from jax import lax
from jax.sharding import PartitionSpec as P

QBR = 256
PBR = 64


LOGIT_SCALE = 50.0
NEG_FILL = -1e30


def inner_rows(first_operand, second_operand):
    return lax.dot_general(
        first_operand, second_operand, (((1,), (1,)), ((), ())), preferred_element_type=jnp.float32
    )


def inner_cols(first_operand, second_operand):
    return lax.dot_general(
        first_operand, second_operand, (((0,), (0,)), ((), ())), preferred_element_type=jnp.float32
    )


def body(query_emb, passage_emb, block_ids, positives):
    section_count = lax.axis_size("sect")
    shard_count = lax.axis_size("pass")
    shard_index = lax.axis_index("pass")
    query_rows, embed_width = query_emb.shape
    passage_rows = passage_emb.shape[0]
    query_blocks = query_rows // QBR
    per_piece = passage_rows // PBR
    local_count = section_count * per_piece
    candidates = section_count * passage_rows
    gathered = lax.all_gather(passage_emb, "sect", axis=0, tiled=True)
    local_ids = jnp.arange(local_count, dtype=jnp.int32)
    global_blocks = (
        local_ids // per_piece * shard_count + shard_index
    ) * per_piece + local_ids % per_piece
    allowed = jnp.any(block_ids[:, :, None] == global_blocks[None, None, :], axis=1)
    allowed_rows = jnp.broadcast_to(
        allowed[:, None, :, None], (query_blocks, QBR, local_count, PBR)
    )
    allowed_rows = allowed_rows.reshape(query_rows, candidates)
    global_rows = (
        global_blocks[:, None] * PBR + jnp.arange(PBR, dtype=jnp.int32)[None, :]
    ).reshape(candidates)
    target = (positives[:, None] == global_rows[None, :]).astype(jnp.float32)
    scores = LOGIT_SCALE * inner_rows(query_emb, gathered)
    local_top = jnp.max(jnp.where(allowed_rows, scores, NEG_FILL), axis=1)
    row_top = lax.pmax(local_top, "pass")
    exp_terms = jnp.where(allowed_rows, jnp.exp(scores - row_top[:, None]), 0.0)
    row_sum = lax.psum(jnp.sum(exp_terms, axis=1), "pass")
    score_grad = (LOGIT_SCALE * (exp_terms / row_sum[:, None] - target)).astype(jnp.bfloat16)
    query_part = jnp.dot(score_grad, gathered, preferred_element_type=jnp.float32)
    pool_part = inner_cols(score_grad, query_emb)
    query_part = query_part.astype(jnp.bfloat16)
    pool_part = pool_part.astype(jnp.bfloat16)
    query_grad = (
        lax.psum_scatter(query_part, "pass", scatter_dimension=1, tiled=True)
        .astype(jnp.float32)
        .astype(jnp.bfloat16)
    )
    pool_grad = (
        lax.psum_scatter(pool_part, ("sect", "qry"), scatter_dimension=0, tiled=True)
        .astype(jnp.float32)
        .astype(jnp.bfloat16)
    )
    return (query_grad, pool_grad)


def solution(mesh):
    return jax.shard_map(
        body,
        mesh=mesh,
        in_specs=(
            P(("sect", "qry"), None),
            P(("sect", "pass"), None),
            P(("sect", "qry"), None),
            P(("sect", "qry")),
        ),
        out_specs=(P(("sect", "qry"), "pass"), P(("sect", "pass", "qry"), None)),
        check_vma=False,
    )
```

profile of v0, /device:TPU:1, one launch (start us, length us, event | category | flops | bytes accessed | tf_op | source)
XLA Modules:
  0.0 329.2 jit_solution(13325460295013534195)
XLA Ops:
  7.2 0.0 copy-start
  7.2 0.0 all-gather.2.cloned.1.call-start
  7.2 0.7 all-gather.2.cloned.1.call-update
  7.9 0.0 reduce-scatter.3.cloned.1.call-start
  8.0 0.1 iota_add_fusion
  8.0 0.1 add.81
  8.1 0.0 copy-done
  8.1 0.2 compare_reduce_fusion
  8.3 0.3 broadcast_in_dim.8
  8.7 2.4 reshape.76
  11.1 88.0 %all-gather.2.cloned.1.call-done = bf16[1024,4096]{1,0:T(8,128)(2,1)} async-done(((bf16[256,4096]{1,0:T(8,128)(2,1)}), bf16[1024,4096]{1,0:T(8,128)(2,1)}) %all-gather.2.cloned.1.call-update) | async-done | bytes 8388624 | tf_op jit(solution)/shard_map/all_gather | solution.py:36
  99.1 8.4 %select_reduce_fusion = (f32[512]{0:T(512)S(1)}, f32[512,1024]{1,0:T(8,128)S(1)}) fusion(pred[512,1024]{1,0:T(32,128)(4,1)S(1)} %reshape.76, bf16[512,4096]{1,0:T(8,128)(2,1)} %param.4, bf16[1024,4096]{1,0:T(8,128)(2,1)} %all-gather.2.cloned.1.call-done), kind=kOutput, calls=%fused_computation.4 | convolution fusion | flops 4296539648 | bytes 15206400 | tf_op jit(solution)/shard_map/dot_general | solution.py:15
  107.5 0.0 copy-start.1
  107.5 24.2 %pmax.7 = f32[512]{0:T(512)S(1)} all-reduce(f32[512]{0:T(512)S(1)} %get-tuple-element.2), channel_id=1, replica_groups=mesh['sect'=4,'pass'=16,'qry'=4] {'pass'}, use_global_device_ids=true, to_apply=%region_2.3 | all-reduce | flops 512 | bytes 4096 | tf_op jit(solution)/shard_map/pmax | solution.py:52
  131.7 0.7 fusion
  132.5 25.7 %psum.7 = f32[512]{0:T(512)S(1)} all-reduce(f32[512]{0:T(512)S(1)} %fusion), channel_id=1, replica_groups=mesh['sect'=4,'pass'=16,'qry'=4] {'pass'}, use_global_device_ids=true, to_apply=%region_4.5 | all-reduce | flops 512 | bytes 4096 | tf_op jit(solution)/shard_map/psum | solution.py:54
  158.1 0.0 copy-done.1
  158.1 10.3 %convolution_convert_fusion.1 = bf16[512,4096]{1,0:T(8,128)(2,1)} fusion(bf16[1024,4096]{1,0:T(8,128)(2,1)} %all-gather.2.cloned.1.call-done, pred[512,1024]{1,0:T(32,128)(4,1)S(1)} %reshape.76, f32[512,1024]{1,0:T(8,128)S(1)} %get-tuple-element.3, s32[1024]{0:T(1024)S(1)} %add.81, f32[512]{0:T(512)S(1)} %psum.7, f32[512]{0:T(512)S(1)} %pmax.7, ...), kind=kOutput, calls=%fused_computation.1 | convolution fusion | flops 4301783040 | bytes 15214592 | tf_op jit(solution)/shard_map/dot_general | solution.py:56
  168.4 0.0 reduce-scatter.3.cloned.1.call-update
  168.4 0.0 reduce-scatter.5.cloned.1.call-start
  168.4 9.5 %convolution_convert_fusion = bf16[1024,4096]{1,0:T(8,128)(2,1)} fusion(bf16[512,4096]{1,0:T(8,128)(2,1)} %param.4, pred[512,1024]{1,0:T(32,128)(4,1)S(1)} %reshape.76, f32[512,1024]{1,0:T(8,128)S(1)} %get-tuple-element.3, s32[1024]{0:T(1024)S(1)} %add.81, f32[512]{0:T(512)S(1)} %psum.7, f32[512]{0:T(512)S(1)} %pmax.7, s32[512]{0:T(512)S(1)} %copy-done.1), kind=kOutput, calls=%fused_computation | convolution fusion | flops 4303880192 | bytes 15214592 | tf_op jit(solution)/shard_map/dot_general | solution.py:21
  177.9 0.0 reduce-scatter.5.cloned.1.call-update
  178.0 49.1 %reduce-scatter.3.cloned.1.call-done = bf16[512,256]{1,0:T(8,128)(2,1)} async-done(((bf16[512,4096]{1,0:T(8,128)(2,1)}), bf16[512,256]{1,0:T(8,128)(2,1)}) %reduce-scatter.3.cloned.1.call-update) | async-done | bytes 262160 | tf_op jit(solution)/shard_map/reduce_scatter | solution.py:61
  227.1 95.6 %reduce-scatter.5.cloned.1.call-done = bf16[64,4096]{1,0:T(8,128)(2,1)} async-done(((bf16[1024,4096]{1,0:T(8,128)(2,1)}), bf16[64,4096]{1,0:T(8,128)(2,1)}) %reduce-scatter.5.cloned.1.call-update) | async-done | bytes 524304 | tf_op jit(solution)/shard_map/reduce_scatter | solution.py:66
  (1 shorter events, 0.0 us)
Async XLA Ops:
  7.2 1.0 copy-start
  7.2 91.9 %all-gather.2.cloned.1.call-start = ((), (), s32[]{:S(2)}) async-start(), calls=%async_computation.2 | async-start | bytes 10485760 | tf_op jit(solution)/shard_map/all_gather | solution.py:36
  7.9 219.2 %reduce-scatter.3.cloned.1.call-start = ((), (), s32[]{:S(2)}) async-start(), calls=%async_computation.3 | async-start | bytes 4456448 | tf_op jit(solution)/shard_map/reduce_scatter | solution.py:61
  107.5 50.6 %copy-start.1 = (s32[512]{0:T(512)S(1)}, s32[512]{0:T(512)}, u32[]{:S(2)}) copy-start(s32[512]{0:T(512)} %param.7) | copy-start | bytes 6148
  168.4 154.3 %reduce-scatter.5.cloned.1.call-start = ((), (), s32[]{:S(2)}) async-start(), calls=%async_computation.4 | async-start | bytes 8912896 | tf_op jit(solution)/shard_map/reduce_scatter | solution.py:66
Sparse Core Ops, SparseCore 0:
  9.8 89.2 all-gather.1
  168.5 58.5 reduce-scatter.2
  231.4 91.2 reduce-scatter.4
where the time goes:
time: 330 us; the launch traced here: 329 us
  waiting for transfers between devices  233 us (71%)
  blocking collectives  49.9 us (15%)
  matrix products  28.2 us (9%)
  between operations  13.8 us (4%)
    reduce_scatter x1, waiting for transfers between devices, body(): lax.psum_scatter(pool_part, ('sect', 'qry'), scatter_dimension=0, tiled=T...  95.6 us
    all_gather x1, waiting for transfers between devices, body(): gathered = lax.all_gather(passage_emb, 'sect', axis=0, tiled=True)  88 us
    reduce_scatter x1, waiting for transfers between devices, body(): lax.psum_scatter(query_part, 'pass', scatter_dimension=1, tiled=True)  49.1 us
    psum x1, blocking collectives, body(): row_sum = lax.psum(jnp.sum(exp_terms, axis=1), 'pass')  25.7 us
    pmax x1, blocking collectives, body(): row_top = lax.pmax(local_top, 'pass')  24.2 us
    dot_general x1, matrix products, body(): jnp.dot(score_grad, gathered, preferred_element_type=jnp.float32)  10.3 us
    dot_general x1, matrix products, inner_cols(): lax.dot_general(first_operand, second_operand, (((0,), (0,)), ((), ())),...  9.5 us
    dot_general x1, matrix products, inner_rows(): lax.dot_general(first_operand, second_operand, (((1,), (1,)), ((), ())),...  8.42 us
  transfers between devices with their start and end apart: 3, of which 3 were waited for; matrix products, arithmetic and copies ran while one was open for 4% of the time, Pallas kernels for 0%

commit v1 on v0

v1 whole, which is shorter than its diff:
```python
import jax
import jax.numpy as jnp
from jax import lax
from jax.experimental import pallas as pl
from jax.experimental.pallas import tpu as pltpu
from jax.sharding import PartitionSpec as P

QBR = 256
LOGIT_SCALE = 50.0
NEG_FILL = -1e30
NEG_TEST = -1e29
MESH = pl.DeviceIdType.MESH
BF = jnp.bfloat16
F32 = jnp.float32
ORDER = (0, 2, 1, 3)


def dot_nn(a, b):
    return lax.dot_general(a, b, (((1,), (0,)), ((), ())), preferred_element_type=F32)


def dot_nt(a, b):
    return lax.dot_general(a, b, (((1,), (1,)), ((), ())), preferred_element_type=F32)


def kernel(
    q_hbm, p_hbm, m_hbm, pos_hbm, qout, pout,
    qb, pb, mb, posb, sown, ssend, srecv, stat, sgt, sg, qp, pp,
    rz, rx0, rx1, fq, fps, fpr, sibs, sibr,
    loc, sib_s, sib_r, mp_s, mp_r, qy_s, qz_s, q_r, py_s, px_s, p_r,
    sx_s, sx_r, st_s, st_r, gt_s, gt_r, gg_s, gg_r,
    rz_s, rz_r, rx0_s, rx0_r, rx1_s, rx1_r, fq_s, fq_r, fp_s, fp_r, fs_s, fs_r,
):
    y = lax.axis_index("sect")
    p = lax.axis_index("pass")
    x = lax.axis_index("qry")
    z = p // 2
    c = p % 2
    o = 1 - c
    yq = y + 1 - 2 * (y % 2)
    yp = 3 - y
    zr, zl = (z + 1) % 8, (z + 7) % 8
    xr, xl = (x + 1) % 4, (x + 3) % 4
    dev_sib = (y, 2 * z + o, x)
    dev_yq = (yq, p, x)
    dev_yp = (yp, p, x)
    dev_z = ((y, 2 * zr + c, x), (y, 2 * zl + c, x))
    dev_x = ((y, p, xr), (y, p, xl))
    sends = []

    def rc(src, dst, ssem, rsem, dev):
        d = pltpu.make_async_remote_copy(
            src_ref=src, dst_ref=dst, send_sem=ssem, recv_sem=rsem, device_id=dev, device_id_type=MESH
        )
        return d

    def send(src, dst, ssem, rsem, dev):
        d = rc(src, dst, ssem, rsem, dev)
        d.start()
        sends.append(d)

    def arrived(dst, ssem, rsem, dev):
        rc(dst, dst, ssem, rsem, dev).wait_recv()

    def cols(k, core):
        return pl.ds(pl.multiple_of((2 * k + core) * 256, 256), 256)

    loads = []
    for k in range(8):
        d = pltpu.make_async_copy(p_hbm.at[:, :, cols(k, c)], pb.at[k, :, 0, c], loc.at[k])
        d.start()
        loads.append(d)
    for k in range(8):
        d = pltpu.make_async_copy(q_hbm.at[:, cols(k, c)], qb.at[k, pl.ds(0, 512)], loc.at[8 + k])
        d.start()
        loads.append(d)
    for i, (a, b) in enumerate(((m_hbm, mb), (pos_hbm, posb))):
        d = pltpu.make_async_copy(a.at[c], b.at[0], loc.at[16 + i])
        d.start()
        loads.append(d)

    barrier = pltpu.get_barrier_semaphore()

    def hello(dev):
        pl.semaphore_signal(barrier, inc=1, device_id=dev, device_id_type=MESH)

    hello(dev_sib)
    hello(dev_yp)
    hello(dev_yq)
    hello(dev_x[0])
    hello(dev_x[1])
    for j in range(1, 8):
        zz = 2 * ((z + j) % 8) + c
        hello((y, zz, x))
        hello((yq, zz, x))
    pl.semaphore_wait(barrier, 19)

    for k in range(8):
        send(p_hbm.at[:, :, cols(k, o)], pb.at[k, :, 0, c], sib_s.at[k], sib_r.at[k], dev_sib)
    for d in loads:
        d.wait()
    for i in ORDER:
        k = 2 * i + z % 2
        send(qb.at[k, pl.ds(0, 512)], qb.at[k, pl.ds(512, 512)], qy_s.at[i], q_r.at[k], dev_yq)
    for i, (a, b) in enumerate(((m_hbm, mb), (pos_hbm, posb))):
        send(a.at[c], b.at[1], mp_s.at[i], mp_r.at[i], dev_yq)
    for k in range(8):
        arrived(pb.at[k, :, 0, o], sib_s.at[k], sib_r.at[k], dev_sib)
    for i in ORDER:
        k = 2 * i + x % 2
        send(pb.at[k, :, 0], pb.at[k, :, 1], py_s.at[i], p_r.at[k], dev_yp)

    for i in ORDER:
        side = i // 2
        k = 2 * i + z % 2
        blk = qb.at[k, pl.ds(512, 512)]
        arrived(blk, qy_s.at[i], q_r.at[k], dev_yq)
        send(blk, blk, qz_s.at[i], q_r.at[k], dev_z[side])
        k = 2 * i + x % 2
        blk = pb.at[k, :, 1]
        arrived(blk, py_s.at[i], p_r.at[k], dev_yp)
        send(blk, blk, px_s.at[i], p_r.at[k], dev_x[side])
    for i in ORDER:
        side = 1 - i // 2
        k = 2 * i + (z + 1) % 2
        arrived(qb.at[k, pl.ds(512, 512)], qz_s.at[i], q_r.at[k], dev_z[side])
        k = 2 * i + (x + 1) % 2
        arrived(pb.at[k, :, 1], px_s.at[i], p_r.at[k], dev_x[side])

    def scores(blk, out):
        def tile(t, carry):
            for s in range(2):
                acc = None
                for k in range(8):
                    a = pb[k, t].reshape(256, 256)
                    b = qb[k, pl.ds(pl.multiple_of(s * 512 + blk * 256, 256), 256)]
                    d = dot_nt(a, b)
                    acc = d if acc is None else acc + d
                out[t, :, s * 256 : s * 256 + 256] = acc
            return carry

        lax.fori_loop(0, 4, tile, 0)

    scores(o, ssend)
    for t in range(4):
        send(ssend.at[t], srecv.at[t], sx_s.at[t], sx_r.at[t], dev_sib)
    scores(c, sown)
    for i, b in enumerate((mb, posb)):
        arrived(b.at[1], mp_s.at[i], mp_r.at[i], dev_yq)

    def rows_of(t):
        r = lax.broadcasted_iota(jnp.int32, (256, 256), 0)
        sec = jnp.where(r // 128 == 0, y, yp)
        blk = (sec * 16 + 2 * z + (r // 64) % 2) * 4 + t
        return blk, blk * 64 + r % 64

    tops = [jnp.full((1, 256), NEG_FILL, F32) for _ in range(2)]
    for t in range(4):
        arrived(srecv.at[t], sx_s.at[t], sx_r.at[t], dev_sib)
        blk, _ = rows_of(t)
        one_hot = (blk == lax.broadcasted_iota(jnp.int32, (256, 256), 1)).astype(BF)
        for s in range(2):
            lanes = slice(s * 256, s * 256 + 256)
            ok = dot_nn(one_hot, mb[s])
            ok = jnp.concatenate([ok, ok], axis=1) > 0.5
            v = LOGIT_SCALE * (sown[t, :, lanes] + srecv[t, :, lanes])
            v = jnp.where(ok, v, NEG_FILL)
            sown[t, :, lanes] = v
            tops[s] = jnp.maximum(tops[s], jnp.max(v, axis=0, keepdims=True))
    sums = [jnp.zeros((1, 256), F32) for _ in range(2)]
    for t in range(4):
        for s in range(2):
            v = sown[t, :, s * 256 : s * 256 + 256]
            e = jnp.where(v > NEG_TEST, jnp.exp(v - tops[s]), 0.0)
            sums[s] = sums[s] + jnp.sum(e, axis=0, keepdims=True)
    for s in range(2):
        for h in range(2):
            lanes = slice(h * 128, h * 128 + 128)
            stat[0, 2 * s + h : 2 * s + h + 1, :] = tops[s][:, lanes]
            stat[0, 4 + 2 * s + h : 5 + 2 * s + h, :] = sums[s][:, lanes]

    for j in range(8):
        zz = 2 * ((z + j) % 8) + c
        if j:
            send(stat.at[0], stat.at[j], st_s.at[j], st_r.at[j], (y, zz, x))
        send(stat.at[0], stat.at[8 + j], st_s.at[8 + j], st_r.at[8 + j], (yq, zz, x))
    for j in range(8):
        zz = 2 * ((z + 8 - j) % 8) + c
        if j:
            arrived(stat.at[j], st_s.at[j], st_r.at[j], (y, zz, x))
        arrived(stat.at[8 + j], st_s.at[8 + j], st_r.at[8 + j], (yq, zz, x))

    def part(j, row):
        if j >= 8:
            row = (row + 2) % 4 + 4 * (row // 4)
        return stat[j, row : row + 1, :]

    row_top, row_inv = [], []
    for s in range(2):
        ts, iv = [], []
        for h in range(2):
            row = 2 * s + h
            top = part(0, row)
            for j in range(1, 16):
                top = jnp.maximum(top, part(j, row))
            tot = jnp.zeros((1, 128), F32)
            for j in range(16):
                tot = tot + part(j, row + 4) * jnp.exp(part(j, row) - top)
            ts.append(top)
            iv.append(LOGIT_SCALE / tot)
        row_top.append(jnp.concatenate(ts, axis=1))
        row_inv.append(jnp.concatenate(iv, axis=1))

    for t in range(4):
        _, row = rows_of(t)
        for s in range(2):
            v = sown[t, :, s * 256 : s * 256 + 256]
            e = jnp.where(v > NEG_TEST, jnp.exp(v - row_top[s]), 0.0)
            hit = row == posb[s, 0:1, :]
            g = e * row_inv[s] - jnp.where(hit, LOGIT_SCALE, 0.0)
            at = pl.ds(pl.multiple_of(s * 512 + c * 256, 256), 256)
            sgt[t, :, at] = g.astype(BF)
            sg[s, c, :, t * 256 : t * 256 + 256] = jnp.transpose(g).astype(BF)
    for s in range(2):
        mine = sg.at[s, c]
        send(mine, mine, gg_s.at[s], gg_r.at[s], dev_sib)
    for s in range(2):
        mine = sgt.at[:, :, pl.ds(pl.multiple_of(s * 512 + c * 256, 256), 256)]
        send(mine, mine, gt_s.at[s], gt_r.at[s], dev_sib)
    for s in range(2):
        arrived(sg.at[s, o], gg_s.at[s], gg_r.at[s], dev_sib)
        theirs = sgt.at[:, :, pl.ds(pl.multiple_of(s * 512 + o * 256, 256), 256)]
        arrived(theirs, gt_s.at[s], gt_r.at[s], dev_sib)

    def dot_q(k):
        def tile(i, carry):
            s, b = i // 2, i % 2
            qp[k, s, b] = dot_nn(sg[s, b], pb[k].reshape(1024, 256)).astype(BF)
            return carry

        lax.fori_loop(0, 4, tile, 0)

    def dot_p(k):
        def tile(t, carry):
            g = dot_nn(sgt[t], qb[k])
            pp[k, t] = g.astype(BF).reshape(2, 2, 64, 256)
            return carry

        lax.fori_loop(0, 4, tile, 0)

    def plus(dst, *srcs):
        v = dst[...].astype(F32)
        for r in srcs:
            v = v + r[...].astype(F32)
        return v

    x2 = (x + 2) % 4

    def pool_first(k):
        dot_p(k)
        for side in range(2):
            send(pp.at[k, x2, side], rx0.at[side, k], rx0_s.at[side, k], rx0_r.at[side, k], dev_x[side])

    def pool_second(k):
        for side, xx in enumerate((xr, xl)):
            back = dev_x[1 - side]
            arrived(rx0.at[side, k], rx0_s.at[side, k], rx0_r.at[side, k], back)
            blk = pp.at[k, xx, side]
            blk[...] = plus(blk, rx0.at[side, k]).astype(BF)
            send(pp.at[k, xx], rx1.at[side, k], rx1_s.at[side, k], rx1_r.at[side, k], dev_x[side])

    def pool_third(k):
        for side in range(2):
            arrived(rx1.at[side, k], rx1_s.at[side, k], rx1_r.at[side, k], dev_x[1 - side])
        fps[k] = plus(pp.at[k, x, 1], rx1.at[0, k, 1], rx1.at[1, k, 1]).astype(BF)
        send(fps.at[k], fpr.at[k], fp_s.at[k], fp_r.at[k], dev_yp)

    k = (z + 4) % 8
    dot_q(k)
    for side in range(2):
        send(qp.at[k, side], rz.at[side, 0, side], rz_s.at[side, 0, side], rz_r.at[side, 0, side], dev_z[side])
    pool_first(0)
    pool_first(1)
    for h in range(1, 4):
        for side in range(2):
            k = (z + 4 - h) % 8 if side == 0 else (z + 4 + h) % 8
            dot_q(k)
            for s in range(2):
                if h > 1 or s == side:
                    came = rz.at[side, h - 1, s]
                    arrived(came, rz_s.at[side, h - 1, s], rz_r.at[side, h - 1, s], dev_z[1 - side])
                    blk = qp.at[k, s]
                    blk[...] = plus(blk, came).astype(BF)
                send(qp.at[k, s], rz.at[side, h, s], rz_s.at[side, h, s], rz_r.at[side, h, s], dev_z[side])
        pool_first(2 * h)
        pool_first(2 * h + 1)
        pool_second(2 * h - 2)
        pool_second(2 * h - 1)
    dot_q(z)
    pool_second(6)
    pool_second(7)
    for k in range(8):
        pool_third(k)
    for s in (1, 0):
        for side in range(2):
            arrived(rz.at[side, 3, s], rz_s.at[side, 3, s], rz_r.at[side, 3, s], dev_z[1 - side])
        if s == 1:
            blk = qp.at[z, 1]
            blk[...] = plus(blk, rz.at[0, 3, 1], rz.at[1, 3, 1]).astype(BF)
            send(blk, fq, fq_s, fq_r, dev_yq)

    for k in range(8):
        arrived(fpr.at[k], fp_s.at[k], fp_r.at[k], dev_yp)
        mine = plus(pp.at[k, x, 0, c], rx1.at[0, k, 0, c], rx1.at[1, k, 0, c], fpr.at[k, c])
        pout[:, cols(k, c)] = mine.astype(BF)
        sibs[k] = plus(pp.at[k, x, 0, o], rx1.at[0, k, 0, o], rx1.at[1, k, 0, o], fpr.at[k, o]).astype(BF)
    send(sibs, sibr, fs_s, fs_r, dev_sib)
    arrived(fq, fq_s, fq_r, dev_yq)
    qout[...] = plus(qp.at[z, 0], rz.at[0, 3, 0], rz.at[1, 3, 0], fq).astype(BF).reshape(512, 256)
    arrived(sibr, fs_s, fs_r, dev_sib)
    for k in range(8):
        pout[:, cols(k, o)] = sibr[k]
    for d in sends:
        d.wait_send()


def body(query_emb, passage_emb, block_ids, positives):
    names = jnp.any(block_ids[:, :, None] == jnp.arange(256, dtype=jnp.int32)[None, None, :], axis=1)
    names = jnp.broadcast_to(names[:, :, None], (2, 256, 128)).astype(BF)
    wanted = jnp.broadcast_to(positives.reshape(2, 1, QBR), (2, 8, QBR))
    anywhere = pl.BlockSpec(memory_space=pl.ANY)
    dma = pltpu.SemaphoreType.DMA
    vm = pltpu.VMEM
    return pl.pallas_call(
        kernel,
        out_shape=(jax.ShapeDtypeStruct((512, 256), BF), jax.ShapeDtypeStruct((64, 4096), BF)),
        in_specs=[anywhere] * 4,
        out_specs=[pl.BlockSpec(memory_space=pltpu.VMEM)] * 2,
        scratch_shapes=[
            vm((8, 1024, 256), BF),
            vm((8, 4, 2, 2, 64, 256), BF),
            vm((2, 256, 128), BF),
            vm((2, 8, 256), jnp.int32),
            vm((4, 256, 512), F32),
            vm((4, 256, 512), F32),
            vm((4, 256, 512), F32),
            vm((16, 8, 128), F32),
            vm((4, 256, 1024), BF),
            vm((2, 2, 256, 1024), BF),
            vm((8, 2, 2, 256, 256), BF),
            vm((8, 4, 2, 2, 64, 256), BF),
            vm((2, 4, 2, 2, 256, 256), BF),
            vm((2, 8, 2, 64, 256), BF),
            vm((2, 8, 2, 2, 64, 256), BF),
            vm((2, 256, 256), BF),
            vm((8, 2, 64, 256), BF),
            vm((8, 2, 64, 256), BF),
            vm((8, 64, 256), BF),
            vm((8, 64, 256), BF),
            dma((18,)), dma((8,)), dma((8,)), dma((2,)), dma((2,)),
            dma((4,)), dma((4,)), dma((8,)), dma((4,)), dma((4,)), dma((8,)),
            dma((4,)), dma((4,)), dma((16,)), dma((16,)), dma((2,)), dma((2,)), dma((2,)), dma((2,)),
            dma((2, 4, 2)), dma((2, 4, 2)), dma((2, 8)), dma((2, 8)), dma((2, 8)), dma((2, 8)),
            dma, dma, dma((8,)), dma((8,)), dma, dma,
        ],
        compiler_params=pltpu.CompilerParams(
            collective_id=0, has_side_effects=True, vmem_limit_bytes=60 * 1024 * 1024
        ),
    )(query_emb, passage_emb.reshape(4, 64, 4096), names, wanted)


def solution(mesh):
    return jax.shard_map(
        body,
        mesh=mesh,
        in_specs=(
            P(("sect", "qry"), None),
            P(("sect", "pass"), None),
            P(("sect", "qry"), None),
            P(("sect", "qry")),
        ),
        out_specs=(P(("sect", "qry"), "pass"), P(("sect", "pass", "qry"), None)),
        check_vma=False,
    )
```

time: 330 us -> 133 us (0.40)
  waiting for transfers between devices: 233 us -> 0 us
  Pallas kernels: 0 us -> 125 us
  blocking collectives: 49.9 us -> 0 us
  matrix products: 28.2 us -> 0 us
  between operations: 13.8 us -> 0.65 us
    reduce_scatter x2 -> x0, waiting for transfers between devices: 145 us -> none  [the longest x1 95.6 us: body(): lax.psum_scatter(pool_part, ('sect', 'qry'), scatter_dimension=0, tiled=T...]
    pallas_call x0 -> x1, Pallas kernels: none -> 125 us  [body(): pl.pallas_call(kernel, out_shape=(jax.ShapeDtypeStruct((512, 256), BF), j...]
    all_gather x1 -> x0, waiting for transfers between devices: 88 us -> none  [body(): gathered = lax.all_gather(passage_emb, 'sect', axis=0, tiled=True)]
    dot_general x3 -> x0, matrix products: 28.2 us -> none  [the longest x1 10.3 us: body(): jnp.dot(score_grad, gathered, preferred_element_type=jnp.float32)]
    psum x1 -> x0, blocking collectives: 25.7 us -> none  [body(): row_sum = lax.psum(jnp.sum(exp_terms, axis=1), 'pass')]
    pmax x1 -> x0, blocking collectives: 24.2 us -> none  [body(): row_top = lax.pmax(local_top, 'pass')]
    unnamed x4 -> x2, local copies, waits for them, and re-layouts: 0.01 us -> 3.54 us
  transfers between devices with their start and end apart: 3 -> 0, of which waited for: 3 -> 0; matrix products, arithmetic and copies ran while one was open for 4% -> 0% of each run, Pallas kernels for 0% -> 0%
where the time goes in v1:
time: 133 us; the launch traced here: 132 us
  Pallas kernels  125 us (94%)
  local copies, waits for them, and re-layouts  5.63 us (4%)
    pallas_call x1, Pallas kernels, body(): pl.pallas_call(kernel, out_shape=(jax.ShapeDtypeStruct((512, 256), BF), j...  125 us
    unnamed x2, local copies, waits for them, and re-layouts  3.54 us

profile of v1, /device:TPU:1, one launch (start us, length us, event | category | flops | bytes accessed | tf_op | source)
XLA Modules:
  0.0 131.9 jit_solution(5427151303464155665)
XLA Ops:
  0.6 0.8 fusion
  1.4 0.7 broadcast_in_dim.7
  2.1 0.6 broadcast_in_dim.8.pos_hbm
  2.7 0.8 broadcast_in_dim.6.m_hbm
  3.5 124.8 %shard_map.59 = (bf16[512,256]{1,0:T(8,128)(2,1)}, bf16[64,4096]{1,0:T(8,128)(2,1)}) custom-call(bf16[512,4096]{1,0:T(8,128)(2,1)} %q_hbm.1, bf16[4,64,4096]{2,1,0:T(8,128)(2,1)} %bitcast.1, bf16[2,256,128]{2,1,0:T(8,128)(2,1)} %broadcast_in_dim.6.m_hbm, s32[2,8,256]{2,1,0:T(8,128)} %broadcast_in_dim.8.pos_hbm), custom_call_target="tpu_custom_call" | custom-call | tf_op jit(solution)/shard_map/pallas_call | solution.py:334
  128.3 1.7 %copy.8 = bf16[512,256]{1,0:T(8,128)(2,1)} copy(bf16[512,256]{1,0:T(8,128)(2,1)} %get-tuple-element.4) | data formatting | bytes 524288
  130.0 1.9 %copy.9 = bf16[64,4096]{1,0:T(8,128)(2,1)} copy(bf16[64,4096]{1,0:T(8,128)(2,1)} %get-tuple-element.5) | data formatting | bytes 1048576
  (1 shorter events, 0.0 us)

commit v2 on v1

--- a/solution.py
+++ b/solution.py
@@ -5,14 +5,14 @@
 from jax.experimental.pallas import tpu as pltpu
 from jax.sharding import PartitionSpec as P
 
-QBR = 256
 LOGIT_SCALE = 50.0
 NEG_FILL = -1e30
 NEG_TEST = -1e29
 MESH = pl.DeviceIdType.MESH
 BF = jnp.bfloat16
 F32 = jnp.float32
-ORDER = (0, 2, 1, 3)
+Q_ORDER = ((0, 0), (0, 1), (1, 0), (1, 1))
+P_ORDER = ((0, 0), (1, 0), (0, 1), (1, 1))
 
 
 def dot_nn(a, b):
@@ -24,8 +24,8 @@
 
 
 def kernel(
-    q_hbm, p_hbm, m_hbm, pos_hbm, qout, pout,
-    qb, pb, mb, posb, sown, ssend, srecv, stat, sgt, sg, qp, pp,
+    q_hbm, p_hbm, ids_hbm, pos_hbm, qout, pout,
+    qb, pb, idsb, posb, sown, ssend, srecv, stat, sgt, sg, qp, pp,
     rz, rx0, rx1, fq, fps, fpr, sibs, sibr,
     loc, sib_s, sib_r, mp_s, mp_r, qy_s, qz_s, q_r, py_s, px_s, p_r,
     sx_s, sx_r, st_s, st_r, gt_s, gt_r, gg_s, gg_r,
@@ -74,8 +74,8 @@
         d = pltpu.make_async_copy(q_hbm.at[:, cols(k, c)], qb.at[k, pl.ds(0, 512)], loc.at[8 + k])
         d.start()
         loads.append(d)
-    for i, (a, b) in enumerate(((m_hbm, mb), (pos_hbm, posb))):
-        d = pltpu.make_async_copy(a.at[c], b.at[0], loc.at[16 + i])
+    for i, (a, b) in enumerate(((ids_hbm, idsb), (pos_hbm, posb))):
+        d = pltpu.make_async_copy(a, b.at[0], loc.at[16 + i])
         d.start()
         loads.append(d)
 
@@ -99,57 +99,100 @@
         send(p_hbm.at[:, :, cols(k, o)], pb.at[k, :, 0, c], sib_s.at[k], sib_r.at[k], dev_sib)
     for d in loads:
         d.wait()
-    for i in ORDER:
-        k = 2 * i + z % 2
-        send(qb.at[k, pl.ds(0, 512)], qb.at[k, pl.ds(512, 512)], qy_s.at[i], q_r.at[k], dev_yq)
-    for i, (a, b) in enumerate(((m_hbm, mb), (pos_hbm, posb))):
-        send(a.at[c], b.at[1], mp_s.at[i], mp_r.at[i], dev_yq)
-    for k in range(8):
-        arrived(pb.at[k, :, 0, o], sib_s.at[k], sib_r.at[k], dev_sib)
-    for i in ORDER:
-        k = 2 * i + x % 2
-        send(pb.at[k, :, 0], pb.at[k, :, 1], py_s.at[i], p_r.at[k], dev_yp)
-
-    for i in ORDER:
-        side = i // 2
-        k = 2 * i + z % 2
-        blk = qb.at[k, pl.ds(512, 512)]
-        arrived(blk, qy_s.at[i], q_r.at[k], dev_yq)
-        send(blk, blk, qz_s.at[i], q_r.at[k], dev_z[side])
-        k = 2 * i + x % 2
-        blk = pb.at[k, :, 1]
-        arrived(blk, py_s.at[i], p_r.at[k], dev_yp)
-        send(blk, blk, px_s.at[i], p_r.at[k], dev_x[side])
-    for i in ORDER:
-        side = 1 - i // 2
-        k = 2 * i + (z + 1) % 2
-        arrived(qb.at[k, pl.ds(512, 512)], qz_s.at[i], q_r.at[k], dev_z[side])
-        k = 2 * i + (x + 1) % 2
-        arrived(pb.at[k, :, 1], px_s.at[i], p_r.at[k], dev_x[side])
-
-    def scores(blk, out):
+
+    def q_unit(k, h):
+        return qb.at[k, pl.ds(512 + 256 * h, 256)]
+
+    def p_unit(k, h):
+        return pb.at[k, :, 1, c if h == 0 else o]
+
+    for u, (j, h) in enumerate(Q_ORDER):
+        k = (z + 4 * j) % 8
+        send(qb.at[k, pl.ds(256 * h, 256)], q_unit(k, h), qy_s.at[u], q_r.at[k, h], dev_yq)
+    for u, (j, h) in enumerate(P_ORDER):
+        k = (x + 4 * j) % 8
+        if u == 2:
+            for i in range(8):
+                arrived(pb.at[i, :, 0, o], sib_s.at[i], sib_r.at[i], dev_sib)
+        send(pb.at[k, :, 0, c if h == 0 else o], p_unit(k, h), py_s.at[u], p_r.at[k, h], dev_yp)
+    for i, (a, b) in enumerate(((ids_hbm, idsb), (pos_hbm, posb))):
+        send(a, b.at[1], mp_s.at[i], mp_r.at[i], dev_yq)
+
+    streams = (
+        (z, ((zr + 6) % 8, (zl + 2) % 8), q_unit, q_r, Q_ORDER, qy_s, qz_s, dev_yq, dev_z),
+        (x, ((xr + 6) % 8, (xl + 2) % 8), p_unit, p_r, P_ORDER, py_s, px_s, dev_yp, dev_x),
+    )
+
+    def forward(st, u):
+        at, passed, unit, recv, order, ysend, rsend, ydev, rdev = st
+        j, h = order[u]
+        k = (at + 4 * j) % 8
+        arrived(unit(k, h), ysend.at[u], recv.at[k, h], ydev)
+        for side in range(2):
+            send(unit(k, h), unit(k, h), rsend.at[side, u], recv.at[k, h], rdev[side])
+
+    def relay(st, h):
+        at, passed, unit, recv, order, ysend, rsend, ydev, rdev = st
+        for side in range(2):
+            k = passed[side]
+            arrived(unit(k, h), rsend.at[side, h], recv.at[k, h], rdev[1 - side])
+            send(unit(k, h), unit(k, h), rsend.at[side, 4 + h], recv.at[k, h], rdev[side])
+
+    def take(st, final):
+        at, passed, unit, recv, order, ysend, rsend, ydev, rdev = st
+        for k in ((at + 6) % 8, (at + 2) % 8) if final else ((passed[0] + 4) % 8, (passed[1] + 4) % 8):
+            for h in range(2):
+                arrived(unit(k, h), ysend.at[0], recv.at[k, h], rdev[0])
+
+    for u in range(4):
+        for st in streams:
+            forward(st, u)
+        if u == 1:
+            for st in streams:
+                relay(st, 0)
+        if u == 3:
+            for st in streams:
+                relay(st, 1)
+    for st in streams:
+        take(st, False)
+
+    def scores(blk, out, ks, more):
         def tile(t, carry):
             for s in range(2):
                 acc = None
-                for k in range(8):
+                for k in ks:
                     a = pb[k, t].reshape(256, 256)
                     b = qb[k, pl.ds(pl.multiple_of(s * 512 + blk * 256, 256), 256)]
                     d = dot_nt(a, b)
                     acc = d if acc is None else acc + d
-                out[t, :, s * 256 : s * 256 + 256] = acc
+                lanes = slice(s * 256, s * 256 + 256)
+                if more:
+                    acc = acc + out[t, :, lanes]
+                out[t, :, lanes] = acc
             return carry
 
         lax.fori_loop(0, 4, tile, 0)
 
-    scores(o, ssend)
+    late = (z + 2) % 4
+    gap = ((x - z + 4) % 4 + 2) % 3 + 1
+    first = (late + jnp.where(gap == 1, 2, 1)) % 4
+    second = (late + jnp.where(gap == 3, 2, 3)) % 4
+    gap = (late + gap) % 4
+    early_ks = (first, first + 4, second, second + 4)
+    late_ks = (late, late + 4, gap, gap + 4)
+    scores(o, ssend, early_ks, False)
+    scores(c, sown, early_ks, False)
+    for st in streams:
+        take(st, True)
+    scores(o, ssend, late_ks, True)
     for t in range(4):
         send(ssend.at[t], srecv.at[t], sx_s.at[t], sx_r.at[t], dev_sib)
-    scores(c, sown)
-    for i, b in enumerate((mb, posb)):
+    scores(c, sown, late_ks, True)
+    for i, b in enumerate((idsb, posb)):
         arrived(b.at[1], mp_s.at[i], mp_r.at[i], dev_yq)
 
-    def rows_of(t):
-        r = lax.broadcasted_iota(jnp.int32, (256, 256), 0)
+    def rows_of(t, lanes):
+        r = lax.broadcasted_iota(jnp.int32, (256, lanes), 0)
         sec = jnp.where(r // 128 == 0, y, yp)
         blk = (sec * 16 + 2 * z + (r // 64) % 2) * 4 + t
         return blk, blk * 64 + r % 64
@@ -157,12 +200,11 @@
     tops = [jnp.full((1, 256), NEG_FILL, F32) for _ in range(2)]
     for t in range(4):
         arrived(srecv.at[t], sx_s.at[t], sx_r.at[t], dev_sib)
-        blk, _ = rows_of(t)
-        one_hot = (blk == lax.broadcasted_iota(jnp.int32, (256, 256), 1)).astype(BF)
+        blk, _ = rows_of(t, 64)
         for s in range(2):
             lanes = slice(s * 256, s * 256 + 256)
-            ok = dot_nn(one_hot, mb[s])
-            ok = jnp.concatenate([ok, ok], axis=1) > 0.5
+            named = jnp.where(blk == idsb[s, pl.ds(c, 1), :], 1.0, 0.0)
+            ok = jnp.broadcast_to(jnp.max(named, axis=1, keepdims=True), (256, 256)) > 0.5
             v = LOGIT_SCALE * (sown[t, :, lanes] + srecv[t, :, lanes])
             v = jnp.where(ok, v, NEG_FILL)
             sown[t, :, lanes] = v
@@ -212,11 +254,12 @@
         row_inv.append(jnp.concatenate(iv, axis=1))
 
     for t in range(4):
-        _, row = rows_of(t)
+        _, row = rows_of(t, 256)
         for s in range(2):
             v = sown[t, :, s * 256 : s * 256 + 256]
             e = jnp.where(v > NEG_TEST, jnp.exp(v - row_top[s]), 0.0)
-            hit = row == posb[s, 0:1, :]
+            want = [posb[s, pl.ds(2 * c + h, 1), :] for h in range(2)]
+            hit = row == jnp.concatenate(want, axis=1)
             g = e * row_inv[s] - jnp.where(hit, LOGIT_SCALE, 0.0)
             at = pl.ds(pl.multiple_of(s * 512 + c * 256, 256), 256)
             sgt[t, :, at] = g.astype(BF)
@@ -325,9 +368,6 @@
 
 
 def body(query_emb, passage_emb, block_ids, positives):
-    names = jnp.any(block_ids[:, :, None] == jnp.arange(256, dtype=jnp.int32)[None, None, :], axis=1)
-    names = jnp.broadcast_to(names[:, :, None], (2, 256, 128)).astype(BF)
-    wanted = jnp.broadcast_to(positives.reshape(2, 1, QBR), (2, 8, QBR))
     anywhere = pl.BlockSpec(memory_space=pl.ANY)
     dma = pltpu.SemaphoreType.DMA
     vm = pltpu.VMEM
@@ -339,8 +379,8 @@
         scratch_shapes=[
             vm((8, 1024, 256), BF),
             vm((8, 4, 2, 2, 64, 256), BF),
-            vm((2, 256, 128), BF),
-            vm((2, 8, 256), jnp.int32),
+            vm((2, 2, 64), jnp.int32),
+            vm((2, 4, 128), jnp.int32),
             vm((4, 256, 512), F32),
             vm((4, 256, 512), F32),
             vm((4, 256, 512), F32),
@@ -358,7 +398,7 @@
             vm((8, 64, 256), BF),
             vm((8, 64, 256), BF),
             dma((18,)), dma((8,)), dma((8,)), dma((2,)), dma((2,)),
-            dma((4,)), dma((4,)), dma((8,)), dma((4,)), dma((4,)), dma((8,)),
+            dma((4,)), dma((2, 6)), dma((8, 2)), dma((4,)), dma((2, 6)), dma((8, 2)),
             dma((4,)), dma((4,)), dma((16,)), dma((16,)), dma((2,)), dma((2,)), dma((2,)), dma((2,)),
             dma((2, 4, 2)), dma((2, 4, 2)), dma((2, 8)), dma((2, 8)), dma((2, 8)), dma((2, 8)),
             dma, dma, dma((8,)), dma((8,)), dma, dma,
@@ -366,7 +406,7 @@
         compiler_params=pltpu.CompilerParams(
             collective_id=0, has_side_effects=True, vmem_limit_bytes=60 * 1024 * 1024
         ),
-    )(query_emb, passage_emb.reshape(4, 64, 4096), names, wanted)
+    )(query_emb, passage_emb.reshape(4, 64, 4096), block_ids, positives.reshape(4, 128))
 
 
 def solution(mesh):

time: 133 us -> 118 us (0.89)
  Pallas kernels: 125 us -> 114 us
  local copies, waits for them, and re-layouts: 5.63 us -> 3.54 us
    pallas_call x1, Pallas kernels: 125 us -> 114 us  [body(): pl.pallas_call(kernel, out_shape=(jax.ShapeDtypeStruct((512, 256), BF), j...]
    broadcast_in_dim x3 -> x0, local copies, waits for them, and re-layouts: 2.1 us -> none  [the longest x2 1.31 us: body(): wanted = jnp.broadcast_to(positives.reshape(2, 1, QBR), (2, 8, QBR))]
where the time goes in v2:
time: 118 us
  Pallas kernels  114 us (97%)
  local copies, waits for them, and re-layouts  3.54 us (3%)
    pallas_call x1, Pallas kernels, body(): pl.pallas_call(kernel, out_shape=(jax.ShapeDtypeStruct((512, 256), BF), j...  114 us
    unnamed x2, local copies, waits for them, and re-layouts  3.54 us

profile of v2, /device:TPU:1, one launch (start us, length us, event | category | flops | bytes accessed | tf_op | source)
XLA Modules:
  0.0 117.8 jit_solution(9263038920697792887)
XLA Ops:
  0.6 113.6 %shard_map.59 = (bf16[512,256]{1,0:T(8,128)(2,1)}, bf16[64,4096]{1,0:T(8,128)(2,1)}) custom-call(bf16[512,4096]{1,0:T(8,128)(2,1)} %q_hbm.1, bf16[4,64,4096]{2,1,0:T(8,128)(2,1)} %bitcast.2, s32[2,64]{1,0:T(2,128)} %ids_hbm.1, s32[4,128]{1,0:T(4,128)} %bitcast.3), custom_call_target="tpu_custom_call" | custom-call | tf_op jit(solution)/shard_map/pallas_call | solution.py:374
  114.3 1.7 %copy.8 = bf16[512,256]{1,0:T(8,128)(2,1)} copy(bf16[512,256]{1,0:T(8,128)(2,1)} %get-tuple-element.4) | data formatting | bytes 524288
  115.9 1.9 %copy.9 = bf16[64,4096]{1,0:T(8,128)(2,1)} copy(bf16[64,4096]{1,0:T(8,128)(2,1)} %get-tuple-element.5) | data formatting | bytes 1048576

commit v3 on v2

--- a/solution.py
+++ b/solution.py
@@ -12,6 +12,7 @@
 BF = jnp.bfloat16
 F32 = jnp.float32
 Q_ORDER = ((0, 0), (0, 1), (1, 0), (1, 1))
+UNITS = ((0, 0), (0, 1), (1, 1))
 P_ORDER = ((0, 0), (1, 0), (0, 1), (1, 1))
 
 
@@ -26,10 +27,10 @@
 def kernel(
     q_hbm, p_hbm, ids_hbm, pos_hbm, qout, pout,
     qb, pb, idsb, posb, sown, ssend, srecv, stat, sgt, sg, qp, pp,
-    rz, rx0, rx1, fq, fps, fpr, sibs, sibr,
+    rz, rx0, rx1, qa, pa, fq, fps, fpr, sibs, sibr,
     loc, sib_s, sib_r, mp_s, mp_r, qy_s, qz_s, q_r, py_s, px_s, p_r,
     sx_s, sx_r, st_s, st_r, gt_s, gt_r, gg_s, gg_r,
-    rz_s, rz_r, rx0_s, rx0_r, rx1_s, rx1_r, fq_s, fq_r, fp_s, fp_r, fs_s, fs_r,
+    qa_s, qa_r, pa_s, pa_r, rz_s, rz_r, rx0_s, rx0_r, rx1_s, rx1_r, fq_s, fq_r, fp_s, fp_r, fs_s, fs_r,
 ):
     y = lax.axis_index("sect")
     p = lax.axis_index("pass")
@@ -272,8 +273,6 @@
         send(mine, mine, gt_s.at[s], gt_r.at[s], dev_sib)
     for s in range(2):
         arrived(sg.at[s, o], gg_s.at[s], gg_r.at[s], dev_sib)
-        theirs = sgt.at[:, :, pl.ds(pl.multiple_of(s * 512 + o * 256, 256), 256)]
-        arrived(theirs, gt_s.at[s], gt_r.at[s], dev_sib)
 
     def dot_q(k):
         def tile(i, carry):
@@ -297,69 +296,161 @@
             v = v + r[...].astype(F32)
         return v
 
+    def query_first(k):
+        dot_q(k)
+        send(qp.at[k, 1, 0], qa.at[k], qa_s.at[k], qa_r.at[k], dev_yq)
+
+    def query_pair(k):
+        arrived(qa.at[k], qa_s.at[k], qa_r.at[k], dev_yq)
+        blk = qp.at[k, 0, 0]
+        blk[...] = plus(blk, qa.at[k]).astype(BF)
+
+    def ring_z(h, u):
+        r, b = UNITS[u]
+        for side in range(2):
+            k = (z + 4 - h) % 8 if side == 0 else (z + 4 + h) % 8
+            half = pl.ds(128 * side, 128)
+            if h == 0:
+                src, dst = qp.at[k, r, b, half], rz.at[side, 0, u, half]
+            else:
+                src, dst = qp.at[k, r, b], rz.at[side, h, u]
+                if h == 1:
+                    came, blk = rz.at[side, 0, u, half], qp.at[k, r, b, half]
+                else:
+                    came, blk = rz.at[side, h - 1, u], src
+                arrived(came, rz_s.at[side, h - 1, u], rz_r.at[side, h - 1, u], dev_z[1 - side])
+                blk[...] = plus(blk, came).astype(BF)
+            send(src, dst, rz_s.at[side, h, u], rz_r.at[side, h, u], dev_z[side])
+
     x2 = (x + 2) % 4
+    rest = pl.ds(1, 2)
 
     def pool_first(k):
         dot_p(k)
-        for side in range(2):
-            send(pp.at[k, x2, side], rx0.at[side, k], rx0_s.at[side, k], rx0_r.at[side, k], dev_x[side])
-
-    def pool_second(k):
+        send(pp.at[k, :, 1, 0], pa.at[k], pa_s.at[k], pa_r.at[k], dev_yp)
+        for side in range(2):
+            src = pp.at[k, x2, :, 1, pl.ds(32 * side, 32)]
+            send(src, rx0.at[side, k, rest], rx0_s.at[side, k, 1], rx0_r.at[side, k, 1], dev_x[side])
+
+    def pool_pair(k):
+        arrived(pa.at[k], pa_s.at[k], pa_r.at[k], dev_yp)
+        blk = pp.at[k, :, 0, 0]
+        blk[...] = plus(blk, pa.at[k]).astype(BF)
+        for side in range(2):
+            src = pp.at[k, x2, 0, 0, pl.ds(32 * side, 32)]
+            send(src, rx0.at[side, k, 0], rx0_s.at[side, k, 0], rx0_r.at[side, k, 0], dev_x[side])
+
+    def pool_second(k, i):
         for side, xx in enumerate((xr, xl)):
-            back = dev_x[1 - side]
-            arrived(rx0.at[side, k], rx0_s.at[side, k], rx0_r.at[side, k], back)
-            blk = pp.at[k, xx, side]
-            blk[...] = plus(blk, rx0.at[side, k]).astype(BF)
-            send(pp.at[k, xx], rx1.at[side, k], rx1_s.at[side, k], rx1_r.at[side, k], dev_x[side])
+            half = pl.ds(32 * side, 32)
+            if i:
+                src, blk, u = pp.at[k, xx, :, 1], pp.at[k, xx, :, 1, half], rest
+            else:
+                src, blk, u = pp.at[k, xx, 0, 0], pp.at[k, xx, 0, 0, half], 0
+            came = rx0.at[side, k, u]
+            arrived(came, rx0_s.at[side, k, i], rx0_r.at[side, k, i], dev_x[1 - side])
+            blk[...] = plus(blk, came).astype(BF)
+            send(src, rx1.at[side, k, u], rx1_s.at[side, k, i], rx1_r.at[side, k, i], dev_x[side])
 
     def pool_third(k):
         for side in range(2):
-            arrived(rx1.at[side, k], rx1_s.at[side, k], rx1_r.at[side, k], dev_x[1 - side])
-        fps[k] = plus(pp.at[k, x, 1], rx1.at[0, k, 1], rx1.at[1, k, 1]).astype(BF)
+            arrived(rx1.at[side, k, rest], rx1_s.at[side, k, 1], rx1_r.at[side, k, 1], dev_x[1 - side])
+        fps[k] = plus(pp.at[k, x, 1, 1], rx1.at[0, k, 2], rx1.at[1, k, 2]).astype(BF)
         send(fps.at[k], fpr.at[k], fp_s.at[k], fp_r.at[k], dev_yp)
 
-    k = (z + 4) % 8
-    dot_q(k)
-    for side in range(2):
-        send(qp.at[k, side], rz.at[side, 0, side], rz_s.at[side, 0, side], rz_r.at[side, 0, side], dev_z[side])
+    def from_z(u):
+        for side in range(2):
+            arrived(rz.at[side, 3, u], rz_s.at[side, 3, u], rz_r.at[side, 3, u], dev_z[1 - side])
+
+    query_first((z + 4) % 8)
+    ring_z(0, 1)
+    ring_z(0, 2)
+    for s in range(2):
+        theirs = sgt.at[:, :, pl.ds(pl.multiple_of(s * 512 + o * 256, 256), 256)]
+        arrived(theirs, gt_s.at[s], gt_r.at[s], dev_sib)
     pool_first(0)
+    query_first((z + 3) % 8)
+    query_first((z + 5) % 8)
+    ring_z(1, 1)
     pool_first(1)
-    for h in range(1, 4):
-        for side in range(2):
-            k = (z + 4 - h) % 8 if side == 0 else (z + 4 + h) % 8
-            dot_q(k)
-            for s in range(2):
-                if h > 1 or s == side:
-                    came = rz.at[side, h - 1, s]
-                    arrived(came, rz_s.at[side, h - 1, s], rz_r.at[side, h - 1, s], dev_z[1 - side])
-                    blk = qp.at[k, s]
-                    blk[...] = plus(blk, came).astype(BF)
-                send(qp.at[k, s], rz.at[side, h, s], rz_s.at[side, h, s], rz_r.at[side, h, s], dev_z[side])
-        pool_first(2 * h)
-        pool_first(2 * h + 1)
-        pool_second(2 * h - 2)
-        pool_second(2 * h - 1)
-    dot_q(z)
-    pool_second(6)
-    pool_second(7)
+    query_pair((z + 4) % 8)
+    ring_z(0, 0)
+    ring_z(1, 2)
+    pool_second(0, 1)
+    pool_first(2)
+    pool_pair(0)
+    query_first((z + 2) % 8)
+    query_first((z + 6) % 8)
+    query_pair((z + 3) % 8)
+    query_pair((z + 5) % 8)
+    ring_z(1, 0)
+    pool_second(1, 1)
+    pool_second(0, 0)
+    pool_first(3)
+    pool_pair(1)
+    ring_z(2, 1)
+    query_first((z + 1) % 8)
+    query_first((z + 7) % 8)
+    pool_second(2, 1)
+    pool_first(4)
+    pool_second(1, 0)
+    pool_pair(2)
+    ring_z(2, 2)
+    query_first(z)
+    pool_first(5)
+    pool_second(3, 1)
+    pool_first(6)
+    query_pair((z + 2) % 8)
+    query_pair((z + 6) % 8)
+    ring_z(2, 0)
+    pool_second(4, 1)
+    pool_first(7)
+    pool_second(2, 0)
+    pool_pair(3)
+    pool_third(0)
+    pool_third(1)
+    pool_second(5, 1)
+    pool_second(3, 0)
+    pool_pair(4)
+    ring_z(3, 2)
+    pool_third(2)
+    pool_third(3)
+    pool_second(6, 1)
+    pool_second(4, 0)
+    pool_pair(5)
+    query_pair((z + 1) % 8)
+    query_pair((z + 7) % 8)
+    ring_z(3, 1)
+    pool_third(4)
+    pool_second(7, 1)
+    pool_second(5, 0)
+    pool_pair(6)
+    pool_third(5)
+    ring_z(3, 0)
+    pool_third(6)
+    pool_second(6, 0)
+    pool_pair(7)
+    pool_third(7)
+    query_pair(z)
+    from_z(2)
+    blk = qp.at[z, 1, 1]
+    blk[...] = plus(blk, rz.at[0, 3, 2], rz.at[1, 3, 2]).astype(BF)
+    send(blk, fq, fq_s, fq_r, dev_yq)
+    pool_second(7, 0)
+
     for k in range(8):
-        pool_third(k)
-    for s in (1, 0):
-        for side in range(2):
-            arrived(rz.at[side, 3, s], rz_s.at[side, 3, s], rz_r.at[side, 3, s], dev_z[1 - side])
-        if s == 1:
-            blk = qp.at[z, 1]
-            blk[...] = plus(blk, rz.at[0, 3, 1], rz.at[1, 3, 1]).astype(BF)
-            send(blk, fq, fq_s, fq_r, dev_yq)
-
-    for k in range(8):
+        for side in range(2):
+            arrived(rx1.at[side, k, 0], rx1_s.at[side, k, 0], rx1_r.at[side, k, 0], dev_x[1 - side])
         arrived(fpr.at[k], fp_s.at[k], fp_r.at[k], dev_yp)
-        mine = plus(pp.at[k, x, 0, c], rx1.at[0, k, 0, c], rx1.at[1, k, 0, c], fpr.at[k, c])
-        pout[:, cols(k, c)] = mine.astype(BF)
-        sibs[k] = plus(pp.at[k, x, 0, o], rx1.at[0, k, 0, o], rx1.at[1, k, 0, o], fpr.at[k, o]).astype(BF)
-    send(sibs, sibr, fs_s, fs_r, dev_sib)
+        sibs[0, k] = plus(pp.at[k, x, 0, 0], rx1.at[0, k, 0], rx1.at[1, k, 0]).astype(BF)
+        sibs[1, k] = plus(pp.at[k, x, 0, 1], rx1.at[0, k, 1], rx1.at[1, k, 1], fpr.at[k]).astype(BF)
+        pout[:, cols(k, c)] = sibs[c, k]
+    send(sibs.at[o], sibr, fs_s, fs_r, dev_sib)
+    from_z(1)
     arrived(fq, fq_s, fq_r, dev_yq)
-    qout[...] = plus(qp.at[z, 0], rz.at[0, 3, 0], rz.at[1, 3, 0], fq).astype(BF).reshape(512, 256)
+    qout[256:512] = plus(qp.at[z, 0, 1], rz.at[0, 3, 1], rz.at[1, 3, 1], fq).astype(BF)
+    from_z(0)
+    qout[0:256] = plus(qp.at[z, 0, 0], rz.at[0, 3, 0], rz.at[1, 3, 0]).astype(BF)
     arrived(sibr, fs_s, fs_r, dev_sib)
     for k in range(8):
         pout[:, cols(k, o)] = sibr[k]
@@ -389,18 +480,21 @@
             vm((2, 2, 256, 1024), BF),
             vm((8, 2, 2, 256, 256), BF),
             vm((8, 4, 2, 2, 64, 256), BF),
-            vm((2, 4, 2, 2, 256, 256), BF),
-            vm((2, 8, 2, 64, 256), BF),
-            vm((2, 8, 2, 2, 64, 256), BF),
-            vm((2, 256, 256), BF),
-            vm((8, 2, 64, 256), BF),
-            vm((8, 2, 64, 256), BF),
+            vm((2, 4, 3, 256, 256), BF),
+            vm((2, 8, 3, 32, 256), BF),
+            vm((2, 8, 3, 64, 256), BF),
+            vm((8, 256, 256), BF),
+            vm((8, 4, 64, 256), BF),
+            vm((256, 256), BF),
             vm((8, 64, 256), BF),
+            vm((8, 64, 256), BF),
+            vm((2, 8, 64, 256), BF),
             vm((8, 64, 256), BF),
             dma((18,)), dma((8,)), dma((8,)), dma((2,)), dma((2,)),
             dma((4,)), dma((2, 6)), dma((8, 2)), dma((4,)), dma((2, 6)), dma((8, 2)),
             dma((4,)), dma((4,)), dma((16,)), dma((16,)), dma((2,)), dma((2,)), dma((2,)), dma((2,)),
-            dma((2, 4, 2)), dma((2, 4, 2)), dma((2, 8)), dma((2, 8)), dma((2, 8)), dma((2, 8)),
+            dma((8,)), dma((8,)), dma((8,)), dma((8,)),
+            dma((2, 4, 3)), dma((2, 4, 3)), dma((2, 8, 2)), dma((2, 8, 2)), dma((2, 8, 2)), dma((2, 8, 2)),
             dma, dma, dma((8,)), dma((8,)), dma, dma,
         ],
         compiler_params=pltpu.CompilerParams(

time: 118 us -> 110 us (0.932)
  Pallas kernels: 114 us -> 105 us
    pallas_call x1, Pallas kernels: 114 us -> 105 us  [body(): pl.pallas_call(kernel, out_shape=(jax.ShapeDtypeStruct((512, 256), BF), j...]
where the time goes in v3:
time: 110 us
  Pallas kernels  105 us (95%)
  local copies, waits for them, and re-layouts  3.54 us (3%)
    pallas_call x1, Pallas kernels, body(): pl.pallas_call(kernel, out_shape=(jax.ShapeDtypeStruct((512, 256), BF), j...  105 us
    unnamed x2, local copies, waits for them, and re-layouts  3.54 us

profile of v3, /device:TPU:1, one launch (start us, length us, event | category | flops | bytes accessed | tf_op | source)
XLA Modules:
  0.0 109.6 jit_solution(5919702787810623054)
XLA Ops:
  0.6 105.4 %shard_map.59 = (bf16[512,256]{1,0:T(8,128)(2,1)}, bf16[64,4096]{1,0:T(8,128)(2,1)}) custom-call(bf16[512,4096]{1,0:T(8,128)(2,1)} %q_hbm.1, bf16[4,64,4096]{2,1,0:T(8,128)(2,1)} %bitcast.2, s32[2,64]{1,0:T(2,128)} %ids_hbm.1, s32[4,128]{1,0:T(4,128)} %bitcast.3), custom_call_target="tpu_custom_call" | custom-call | tf_op jit(solution)/shard_map/pallas_call | solution.py:465
  106.0 1.7 %copy.8 = bf16[512,256]{1,0:T(8,128)(2,1)} copy(bf16[512,256]{1,0:T(8,128)(2,1)} %get-tuple-element.4) | data formatting | bytes 524288
  107.7 1.9 %copy.9 = bf16[64,4096]{1,0:T(8,128)(2,1)} copy(bf16[64,4096]{1,0:T(8,128)(2,1)} %get-tuple-element.5) | data formatting | bytes 1048576

commit v4 on v3

--- a/solution.py
+++ b/solution.py
@@ -254,18 +254,17 @@
         row_top.append(jnp.concatenate(ts, axis=1))
         row_inv.append(jnp.concatenate(iv, axis=1))
 
-    for t in range(4):
-        _, row = rows_of(t, 256)
-        for s in range(2):
+    for s in range(2):
+        want = [posb[s, pl.ds(2 * c + h, 1), :] for h in range(2)]
+        want = jnp.concatenate(want, axis=1)
+        at = pl.ds(pl.multiple_of(s * 512 + c * 256, 256), 256)
+        for t in range(4):
+            _, row = rows_of(t, 256)
             v = sown[t, :, s * 256 : s * 256 + 256]
             e = jnp.where(v > NEG_TEST, jnp.exp(v - row_top[s]), 0.0)
-            want = [posb[s, pl.ds(2 * c + h, 1), :] for h in range(2)]
-            hit = row == jnp.concatenate(want, axis=1)
-            g = e * row_inv[s] - jnp.where(hit, LOGIT_SCALE, 0.0)
-            at = pl.ds(pl.multiple_of(s * 512 + c * 256, 256), 256)
+            g = e * row_inv[s] - jnp.where(row == want, LOGIT_SCALE, 0.0)
             sgt[t, :, at] = g.astype(BF)
             sg[s, c, :, t * 256 : t * 256 + 256] = jnp.transpose(g).astype(BF)
-    for s in range(2):
         mine = sg.at[s, c]
         send(mine, mine, gg_s.at[s], gg_r.at[s], dev_sib)
     for s in range(2):

time: 110 us -> 109 us (level)
  no operation moved by 1% of the time
where the time goes in v4:
time: 109 us
  Pallas kernels  105 us (96%)
  local copies, waits for them, and re-layouts  3.54 us (3%)
    pallas_call x1, Pallas kernels, body(): pl.pallas_call(kernel, out_shape=(jax.ShapeDtypeStruct((512, 256), BF), j...  105 us
    unnamed x2, local copies, waits for them, and re-layouts  3.54 us

profile of v4, /device:TPU:1, one launch (start us, length us, event | category | flops | bytes accessed | tf_op | source)
XLA Modules:
  0.0 109.1 jit_solution(8105865306870473368)
XLA Ops:
  0.6 105.0 %shard_map.59 = (bf16[512,256]{1,0:T(8,128)(2,1)}, bf16[64,4096]{1,0:T(8,128)(2,1)}) custom-call(bf16[512,4096]{1,0:T(8,128)(2,1)} %q_hbm.1, bf16[4,64,4096]{2,1,0:T(8,128)(2,1)} %bitcast.2, s32[2,64]{1,0:T(2,128)} %ids_hbm.1, s32[4,128]{1,0:T(4,128)} %bitcast.3), custom_call_target="tpu_custom_call" | custom-call | tf_op jit(solution)/shard_map/pallas_call | solution.py:464
  105.6 1.7 %copy.8 = bf16[512,256]{1,0:T(8,128)(2,1)} copy(bf16[512,256]{1,0:T(8,128)(2,1)} %get-tuple-element.4) | data formatting | bytes 524288
  107.3 1.9 %copy.9 = bf16[64,4096]{1,0:T(8,128)(2,1)} copy(bf16[64,4096]{1,0:T(8,128)(2,1)} %get-tuple-element.5) | data formatting | bytes 1048576
